TPU v7x, 32 devices: a whole 2x2x4 slice. The times are simulated.
32 devices in a mesh: fsdp: 4 (over y, x), ctx: 4 (over z), tensor: 2 (over core).
Axes of the slice: x: 2, y: 2, z: 4, core: 2. Of those that a mesh axis runs over, the one named last changes fastest.
Arguments:
- layer_input: bfloat16 [8, 1024, 768], P(('fsdp', 'tensor'), 'ctx'), may hold values from -6 to 6
- cotangent: bfloat16 [8, 1024, 768], P(('fsdp', 'tensor'), 'ctx'), may hold values from -6 to 6
- segment_ids: int32 [8, 1024], P(('fsdp', 'tensor'), 'ctx'), may hold values from 0 to 5, as said below
- positions: int32 [8, 1024], P(('fsdp', 'tensor'), 'ctx'), may hold values from 0 to 1023, as said below
- query_key_value_weight: bfloat16 [768, 2304], P('fsdp'), may hold values from -0.21875 to 0.21875
- projection_matrix: bfloat16 [768, 768], P('fsdp'), may hold values from -0.875 to 0.875
- up_matrix: bfloat16 [768, 3072], P('fsdp', 'tensor'), may hold values from -0.21875 to 0.21875
- down_matrix: bfloat16 [3072, 768], P('tensor', 'fsdp'), may hold values from -0.109375 to 0.109375
- attn_gain: bfloat16 [768], P('fsdp'), may hold values from 0.5 to 1.5
- attn_shift: bfloat16 [768], P('fsdp'), may hold values from -3 to 3
- ffn_gain: bfloat16 [768], P('fsdp'), may hold values from 0.5 to 1.5
- ffn_shift: bfloat16 [768], P('fsdp'), may hold values from -3 to 3
- out_bias: bfloat16 [768], P('fsdp'), may hold values from -3 to 3
- up_projection_bias: bfloat16 [3072], P('fsdp'), may hold values from -3 to 3
Outputs:
- layer_output: bfloat16 [8, 1024, 768], P(('fsdp', 'tensor'), 'ctx')
- input_grad: float32 [8, 1024, 768], P(('fsdp', 'tensor'), 'ctx')
- qkv_grad: float32 [768, 2304], P('fsdp')
- proj_grad: float32 [768, 768], P('fsdp')
- up_grad: float32 [768, 3072], P('fsdp', 'tensor')
- down_grad: float32 [3072, 768], P('tensor', 'fsdp')
- attn_gain_grad: float32 [768], P('fsdp')
- attn_shift_grad: float32 [768], P('fsdp')
- ffn_gain_grad: float32 [768], P('fsdp')
- ffn_shift_grad: float32 [768], P('fsdp')
- out_bias_grad: float32 [768], P('fsdp')
- up_bias_grad: float32 [3072], P('fsdp')
Inputs may be any that keep to these rules, and one draw needn't show every extreme that they name: `segment_ids`: along each sequence the ids start at 0 and rise by one at each document's first token; every document has 200 to 1024 tokens, except the last one of a sequence, which the sequence's end may cut. `positions`: each document's tokens count 0, 1, 2, ... from its first token, which starts with the segment_ids' change.
All inputs are finite; a program needn't handle non-finite values.
Results may differ from a plain program's by a relative error of at most 0.018.
Values may be sent and summed in bfloat16 or wider, within the bound.
No kernel may reach another device: no remote copies, remote signals or barrier semaphores. Data moves between devices by JAX's collectives and lax.ppermute only.
A program may use at most 192 MiB of HBM per device.

v0:
```python
import math
import jax
import jax.numpy as jnp
from jax import lax
from jax.sharding import PartitionSpec as P

HEADS = 12
HEAD = 64
ROT = 16
FF = 3072
epsilon = 1e-05
masked_score = -1e30


def normalize(values):
    center = jnp.mean(values, axis=-1, keepdims=True)
    shifted = values - center
    spread = jnp.mean(shifted * shifted, axis=-1, keepdims=True)
    inverse = lax.rsqrt(spread + epsilon)
    return (shifted * inverse, inverse)


def norm_back(grad_hidden, normed, inverse, gain_vec):
    scaled = grad_hidden * gain_vec
    first_mean = jnp.mean(scaled, axis=-1, keepdims=True)
    second_mean = jnp.mean(scaled * normed, axis=-1, keepdims=True)
    return inverse * (scaled - first_mean - normed * second_mean)


def rotary_tables(positions):
    half_rot = ROT // 2
    frequency = 10000.0 ** (-(2.0 * jnp.arange(half_rot, dtype=jnp.float32)) / ROT)
    angles = positions.astype(jnp.float32)[..., None] * frequency
    return (jnp.cos(angles), jnp.sin(angles))


def rotate(fields, cosine, sine_tab):
    half_rot = ROT // 2
    first_half = fields[..., :half_rot]
    second = fields[..., half_rot:ROT]
    return jnp.concatenate(
        [
            first_half * cosine - second * sine_tab,
            second * cosine + first_half * sine_tab,
            fields[..., ROT:],
        ],
        axis=-1,
    )


def unrotate(fields, cosine, sine_tab):
    half_rot = ROT // 2
    first_half = fields[..., :half_rot]
    second = fields[..., half_rot:ROT]
    return jnp.concatenate(
        [
            first_half * cosine + second * sine_tab,
            second * cosine - first_half * sine_tab,
            fields[..., ROT:],
        ],
        axis=-1,
    )


def exact_gelu(values):
    return jax.nn.gelu(values, approximate=False)


def to_tokens(blocks):
    return lax.all_to_all(blocks, "ctx", split_axis=1, concat_axis=3, tiled=True)


def tensor_total(terms):
    return lax.psum_scatter(
        terms.astype(jnp.bfloat16), "tensor", scatter_dimension=0, tiled=True
    ).astype(jnp.float32)


def shards(
    layer_input,
    cotangent,
    segment_ids,
    positions,
    query_key_value_weight,
    projection_matrix,
    up_matrix,
    down_matrix,
    attn_gain,
    attn_shift,
    ffn_gain,
    ffn_shift,
    out_bias,
    up_projection_bias,
):
    ctx_size = lax.axis_size("ctx")
    tensor_size = lax.axis_size("tensor")
    seq_count, piece_len, model_width = layer_input.shape
    token_count = seq_count * piece_len
    ffn_share = FF // tensor_size
    (
        full_qkv,
        full_proj,
        up_share,
        down_share,
        gain_one,
        shift_one,
        gain_two,
        shift_two,
        bias_all,
        up_bias_all,
    ) = (
        lax.all_gather(query_key_value_weight, "fsdp", axis=0, tiled=True),
        lax.all_gather(projection_matrix, "fsdp", axis=0, tiled=True),
        lax.all_gather(up_matrix, "fsdp", axis=0, tiled=True),
        lax.all_gather(down_matrix, "fsdp", axis=1, tiled=True),
        lax.all_gather(attn_gain, "fsdp", axis=0, tiled=True),
        lax.all_gather(attn_shift, "fsdp", axis=0, tiled=True),
        lax.all_gather(ffn_gain, "fsdp", axis=0, tiled=True),
        lax.all_gather(ffn_shift, "fsdp", axis=0, tiled=True),
        lax.all_gather(out_bias, "fsdp", axis=0, tiled=True),
        lax.all_gather(up_projection_bias, "fsdp", axis=0, tiled=True),
    )
    gain_one = gain_one.astype(jnp.float32)
    shift_one = shift_one.astype(jnp.float32)
    gain_two = gain_two.astype(jnp.float32)
    shift_two = shift_two.astype(jnp.float32)
    up_bias_f = up_bias_all.astype(jnp.float32)
    inputs = layer_input.reshape(token_count, model_width).astype(jnp.float32)
    normed, inverse = normalize(inputs)
    first_hidden = (normed * gain_one + shift_one).astype(jnp.bfloat16)
    second_hidden = (normed * gain_two + shift_two).astype(jnp.bfloat16)
    projected_output = jnp.dot(first_hidden, full_qkv, preferred_element_type=jnp.float32).reshape(
        token_count, 3, HEADS, HEAD
    )
    cosine, sine_tab = rotary_tables(positions.reshape(token_count))
    cosine = cosine[:, None, :]
    sine_tab = sine_tab[:, None, :]
    query_tok = rotate(projected_output[:, 0], cosine, sine_tab).astype(jnp.bfloat16)
    key_tok = rotate(projected_output[:, 1], cosine, sine_tab).astype(jnp.bfloat16)
    value_tok = projected_output[:, 2].astype(jnp.bfloat16)
    packed = jnp.stack([query_tok, key_tok, value_tok], axis=1).reshape(
        seq_count, piece_len, 3, HEADS, HEAD
    )
    seg_send = jnp.broadcast_to(
        segment_ids.astype(jnp.bfloat16)[:, :, None, None], (seq_count, piece_len, 1, ctx_size)
    )
    headed, seg_heads = (
        lax.all_to_all(packed, "ctx", split_axis=3, concat_axis=1, tiled=True),
        lax.all_to_all(seg_send, "ctx", split_axis=3, concat_axis=1, tiled=True),
    )
    seq_len = headed.shape[1]
    seg_full = seg_heads.reshape(seq_count, seq_len)
    query_all = headed[:, :, 0]
    key_all = headed[:, :, 1]
    value_all = headed[:, :, 2]
    block_rows = min(512, seq_len)
    scale = math.sqrt(HEAD)

    def block_scores(row_start):
        query_block = lax.dynamic_slice_in_dim(query_all, row_start, block_rows, 1)
        scores = (
            jnp.einsum("sqhe,skhe->shqk", query_block, key_all, preferred_element_type=jnp.float32)
            / scale
        )
        row_ids = row_start + jnp.arange(block_rows)
        col_ids = jnp.arange(seq_len)
        causal = col_ids[None, :] <= row_ids[:, None]
        seg_rows = lax.dynamic_slice_in_dim(seg_full, row_start, block_rows, 1)
        same_doc = seg_rows[:, :, None] == seg_full[:, None, :]
        allowed = (same_doc & causal[None])[:, None]
        return (query_block, jnp.where(allowed, scores, masked_score), allowed)

    context_parts = []
    log_totals = []
    for row_start in range(0, seq_len, block_rows):
        query_block, masked, allowed = block_scores(row_start)
        row_peak = jnp.max(masked, axis=-1, keepdims=True)
        exp_terms = jnp.exp(masked - row_peak)
        row_total = jnp.sum(exp_terms, axis=-1, keepdims=True)
        attn_probs = (exp_terms / row_total).astype(jnp.bfloat16)
        log_totals.append(row_peak + jnp.log(row_total))
        context_parts.append(
            jnp.einsum(
                "shqk,skhe->sqhe", attn_probs, value_all, preferred_element_type=jnp.float32
            ).astype(jnp.bfloat16)
        )
    context_rows = jnp.concatenate(context_parts, axis=1)
    context_tok = to_tokens(context_rows[:, :, None]).reshape(token_count, model_width)
    attention_branch = jnp.dot(context_tok, full_proj, preferred_element_type=jnp.float32)
    grad_bf = cotangent.reshape(token_count, model_width)
    rows_two, rows_grad = (
        lax.all_gather(
            second_hidden.reshape(seq_count, piece_len, model_width), "tensor", axis=0, tiled=True
        ),
        lax.all_gather(cotangent, "tensor", axis=0, tiled=True),
    )
    rows_two = rows_two.reshape(-1, model_width)
    rows_grad = rows_grad.reshape(-1, model_width)
    offset = lax.axis_index("tensor") * ffn_share
    bias_share = lax.dynamic_slice_in_dim(up_bias_f, offset, ffn_share, 0)
    preactivation = jnp.dot(rows_two, up_share, preferred_element_type=jnp.float32) + bias_share
    activated_hidden, gelu_back = jax.vjp(exact_gelu, preactivation)
    act_bf = activated_hidden.astype(jnp.bfloat16)
    feed_part = jnp.dot(act_bf, down_share, preferred_element_type=jnp.float32).reshape(
        tensor_size * seq_count, piece_len, model_width
    )
    feedforward_output = tensor_total(feed_part).reshape(token_count, model_width)
    grad_act = jnp.einsum("td,fd->tf", rows_grad, down_share, preferred_element_type=jnp.float32)
    grad_pre = gelu_back(grad_act)[0].astype(jnp.bfloat16)
    back_part = jnp.einsum(
        "tf,df->td", grad_pre, up_share, preferred_element_type=jnp.float32
    ).reshape(tensor_size * seq_count, piece_len, model_width)
    grad_two = tensor_total(back_part).reshape(token_count, model_width)
    up_part = jnp.einsum("tf,td->fd", grad_pre, rows_two, preferred_element_type=jnp.float32)
    down_part = jnp.einsum("tf,td->fd", act_bf, rows_grad, preferred_element_type=jnp.float32)
    ffn_grad = jnp.stack([up_part, down_part], axis=1)
    up_bias_grad = lax.dynamic_update_slice_in_dim(
        jnp.zeros((FF,), jnp.float32), jnp.sum(grad_pre, axis=0, dtype=jnp.float32), offset, 0
    )
    output = inputs + attention_branch + feedforward_output + bias_all.astype(jnp.float32)
    layer_output = output.astype(jnp.bfloat16).reshape(seq_count, piece_len, model_width)
    grad_context = jnp.einsum(
        "td,cd->tc", grad_bf, full_proj, preferred_element_type=jnp.float32
    ).astype(jnp.bfloat16)
    grad_heads = lax.all_to_all(
        grad_context.reshape(seq_count, piece_len, 1, HEADS, HEAD),
        "ctx",
        split_axis=3,
        concat_axis=1,
        tiled=True,
    )[:, :, 0]
    grad_key = jnp.zeros(key_all.shape, jnp.float32)
    grad_value = jnp.zeros(value_all.shape, jnp.float32)
    query_parts = []
    for part_index, row_start in enumerate(range(0, seq_len, block_rows)):
        query_block, masked, allowed = block_scores(row_start)
        grad_block = lax.dynamic_slice_in_dim(grad_heads, row_start, block_rows, 1)
        full_probs = jnp.where(allowed, jnp.exp(masked - log_totals[part_index]), 0.0)
        grad_probs = jnp.einsum(
            "sqhe,skhe->shqk", grad_block, value_all, preferred_element_type=jnp.float32
        )
        row_delta = jnp.sum(full_probs * grad_probs, axis=-1, keepdims=True)
        grad_scores = (full_probs * (grad_probs - row_delta)).astype(jnp.bfloat16)
        query_parts.append(
            jnp.einsum("shqk,skhe->sqhe", grad_scores, key_all, preferred_element_type=jnp.float32)
            / scale
        )
        grad_key = (
            grad_key
            + jnp.einsum(
                "shqk,sqhe->skhe", grad_scores, query_block, preferred_element_type=jnp.float32
            )
            / scale
        )
        grad_value = grad_value + jnp.einsum(
            "shqk,sqhe->skhe",
            full_probs.astype(jnp.bfloat16),
            grad_block,
            preferred_element_type=jnp.float32,
        )
    grad_query = jnp.concatenate(query_parts, axis=1)
    grad_stack = jnp.stack([grad_query, grad_key, grad_value], axis=2).astype(jnp.bfloat16)
    grad_tok = to_tokens(grad_stack).reshape(token_count, 3, HEADS, HEAD).astype(jnp.float32)
    grad_proj = jnp.stack(
        [
            unrotate(grad_tok[:, 0], cosine, sine_tab),
            unrotate(grad_tok[:, 1], cosine, sine_tab),
            grad_tok[:, 2],
        ],
        axis=1,
    )
    grad_proj = grad_proj.reshape(token_count, 3 * model_width).astype(jnp.bfloat16)
    grad_one = jnp.einsum("tc,dc->td", grad_proj, full_qkv, preferred_element_type=jnp.float32)
    cot_float = grad_bf.astype(jnp.float32)
    input_grad = (
        cot_float
        + norm_back(grad_one, normed, inverse, gain_one)
        + norm_back(grad_two, normed, inverse, gain_two)
    )
    qkv_part = jnp.einsum("tr,tc->rc", first_hidden, grad_proj, preferred_element_type=jnp.float32)
    proj_part = jnp.einsum("tr,tc->rc", context_tok, grad_bf, preferred_element_type=jnp.float32)
    attn_grad = lax.psum_scatter(
        jnp.concatenate([qkv_part, proj_part], axis=1).astype(jnp.bfloat16),
        "fsdp",
        scatter_dimension=0,
        tiled=True,
    )
    small_grad = jnp.stack(
        [
            jnp.sum(grad_one * normed, axis=0),
            jnp.sum(grad_one, axis=0),
            jnp.sum(grad_two * normed, axis=0),
            jnp.sum(grad_two, axis=0),
            jnp.sum(cot_float, axis=0),
        ]
    )
    ffn_part, small_part, bias_part = (
        lax.psum_scatter(
            ffn_grad.astype(jnp.bfloat16), "fsdp", scatter_dimension=2, tiled=True
        ).astype(jnp.float32),
        lax.psum_scatter(
            small_grad.astype(jnp.bfloat16), "fsdp", scatter_dimension=1, tiled=True
        ).astype(jnp.float32),
        lax.psum_scatter(
            up_bias_grad.astype(jnp.bfloat16), "fsdp", scatter_dimension=0, tiled=True
        ).astype(jnp.float32),
    )
    attn_sum, small_sum, bias_sum = (
        lax.psum(attn_grad, ("ctx", "tensor")).astype(jnp.float32),
        lax.psum(small_part.astype(jnp.bfloat16), ("ctx", "tensor")).astype(jnp.float32),
        lax.psum(bias_part.astype(jnp.bfloat16), ("ctx", "tensor")).astype(jnp.float32),
    )
    ffn_sum = lax.psum(ffn_part.astype(jnp.bfloat16), "ctx").astype(jnp.float32)
    return (
        layer_output,
        input_grad.reshape(seq_count, piece_len, model_width),
        attn_sum[:, : 3 * model_width],
        attn_sum[:, 3 * model_width :],
        ffn_sum[:, 0, :].T,
        ffn_sum[:, 1, :],
        small_sum[0],
        small_sum[1],
        small_sum[2],
        small_sum[3],
        small_sum[4],
        bias_sum,
    )


def solution(mesh):
    placed = (
        P(("fsdp", "tensor"), "ctx", None),
        P(("fsdp", "tensor"), "ctx", None),
        P(("fsdp", "tensor"), "ctx"),
        P(("fsdp", "tensor"), "ctx"),
        P("fsdp", None),
        P("fsdp", None),
        P("fsdp", "tensor"),
        P("tensor", "fsdp"),
        P("fsdp"),
        P("fsdp"),
        P("fsdp"),
        P("fsdp"),
        P("fsdp"),
        P("fsdp"),
    )
    return jax.shard_map(
        shards,
        mesh=mesh,
        in_specs=placed,
        out_specs=(
            P(("fsdp", "tensor"), "ctx", None),
            P(("fsdp", "tensor"), "ctx", None),
            P("fsdp", None),
            P("fsdp", None),
            P("fsdp", "tensor"),
            P("tensor", "fsdp"),
            P("fsdp"),
            P("fsdp"),
            P("fsdp"),
            P("fsdp"),
            P("fsdp"),
            P("fsdp"),
        ),
        check_vma=False,
    )
```

profile of v0, /device:TPU:0, one launch (start us, length us, event | category | flops | bytes accessed | tf_op | source)
XLA Modules:
  0.0 541.3 jit_solution(9679620210667269703)
XLA Ops:
  13.8 11.5 %all-reduce.9 = (bf16[768]{0:T(1024)(128)(2,1)S(1)}, bf16[768]{0:T(1024)(128)(2,1)S(1)}) all-reduce(bf16[768]{0:T(1024)(128)(2,1)S(1)} %dynamic-update-slice.3, bf16[768]{0:T(1024)(128)(2,1)S(1)} %dynamic-update-slice.2), channel_id=1, replica_groups=mesh['fsdp'=4,'ctx'=4,'tensor'=2] {'fsdp'}, use_global_device_ids=true, to_apply=%add.3 | all-reduce | flops 1536 | bytes 6144
  26.0 7.2 %all-gather = bf16[4,1,768]{2,1,0:T(2,128)(2,1)S(1)} all-gather(bf16[1,1,768]{2,1,0:T(2,128)(2,1)S(1)} %reshape.746), channel_id=1, replica_groups=mesh['fsdp'=4,'ctx'=4,'tensor'=2] {'fsdp'}, dimensions={0}, use_global_device_ids=true | all-gather | bytes 7680 | tf_op jit(solution)/shard_map/all_gather | solution.py:121
  35.0 2.4 all_gather.42
  37.4 2.4 all_gather.47
  39.7 10.2 %all-gather.10.cloned.1.call-done = bf16[768,1536]{1,0:T(8,128)(2,1)} async-done(((bf16[192,1536]{1,0:T(8,128)(2,1)}), bf16[768,1536]{1,0:T(8,128)(2,1)}) %all-gather.10.cloned.1.call-update) | async-done | bytes 2359312 | tf_op jit(solution)/shard_map/all_gather | solution.py:114
  50.0 11.0 %multiply_convert_fusion.2 = (bf16[512,1536]{1,0:T(8,128)(2,1)}, f32[512,1536]{1,0:T(8,128)}, f32[512,1536]{1,0:T(8,128)}) fusion(f32[1536]{0:T(1024)S(1)} %dynamic_slice.29, bf16[512,768]{1,0:T(8,128)(2,1)S(1)} %bitcast.296, bf16[768,1536]{1,0:T(8,128)(2,1)} %all-gather.10.cloned.1.call-done), kind=kOutput, calls=%fused_computation.30 | convolution fusion | flops 1259864064 | bytes 11016192 | tf_op jit(solution)/shard_map/dot_general | solution.py:201
  61.0 28.2 %all-gather.12.cloned.1.call-done = bf16[1536,768]{0,1:T(8,128)(2,1)} async-done(((bf16[1536,192]{0,1:T(8,128)(2,1)}), bf16[1536,768]{0,1:T(8,128)(2,1)}) %all-gather.12.cloned.1.call-update) | async-done | bytes 2359312 | tf_op jit(solution)/shard_map/all_gather | solution.py:115
  89.2 5.9 %convert_reduce_fusion = (bf16[1536]{0:T(1024)(128)(2,1)S(1)}, bf16[512,1536]{1,0:T(8,128)(2,1)S(1)}) fusion(f32[512,1536]{1,0:T(8,128)} %get-tuple-element.57, f32[512,1536]{1,0:T(8,128)} %get-tuple-element.91, bf16[512,768]{1,0:T(8,128)(2,1)S(1)} %bitcast.294, bf16[1536,768]{0,1:T(8,128)(2,1)} %all-gather.12.cloned.1.call-done), kind=kOutput, calls=%fused_computation.24 | convolution fusion | flops 1220540928 | bytes 11013120 | tf_op jit(solution)/shard_map/td,fd->tf/dot_general | solution.py:208
  95.1 2.3 convolution_convert_fusion.4
  97.5 3.0 fusion.16
  101.9 2.5 pad_maximum_fusion.1
  104.5 12.7 %copy.65 = bf16[1536,2,768]{0,1,2:T(2,128)(2,1)} copy(bf16[1536,2,768]{2,0,1:T(8,128)(2,1)} %pad_maximum_fusion.1) | data formatting | bytes 9437184 | tf_op jit(solution)/shard_map/stack | solution.py:216
  119.7 4.7 all-to-all-start.1
  128.8 16.1 %all-reduce.8 = (bf16[768]{0:T(1024)(128)(2,1)S(1)}, bf16[768]{0:T(1024)(128)(2,1)S(1)}, bf16[3072]{0:T(1024)(128)(2,1)}, bf16[768]{0:T(1024)(128)(2,1)}) all-reduce(bf16[768]{0:T(1024)(128)(2,1)S(1)} %dynamic-update-slice.1, bf16[768]{0:T(1024)(128)(2,1)S(1)} %dynamic-update-slice, ...), channel_id=1, replica_groups=mesh['fsdp'=4,'ctx'=4,'tensor'=2] {'fsdp'}, use_global_device_ids=true, to_apply=%add.1 | all-reduce | flops 5376 | bytes 21504
  144.9 22.7 %all-gather.6.cloned.1.call-done = bf16[768,2304]{1,0:T(8,128)(2,1)} async-done(((bf16[192,2304]{1,0:T(8,128)(2,1)}), bf16[768,2304]{1,0:T(8,128)(2,1)}) %all-gather.6.cloned.1.call-update) | async-done | bytes 3538960 | tf_op jit(solution)/shard_map/all_gather | solution.py:112
  167.6 4.5 copy.53
  172.2 2.3 fusion.73
  174.7 4.6 all-to-all-start.3
  180.7 10.1 %all-to-all-done.3 = bf16[1,256,1,12,64]{1,4,2,0,3:T(8,128)(2,1)S(1)} async-done(((bf16[1,256,1,12,64]{1,4,2,0,3:T(8,128)(2,1)}), bf16[1,256,1,12,64]{1,4,2,0,3:T(8,128)(2,1)S(1)}, u32[]{:S(2)}, u32[]{:S(2)}) %all-to-all-start.3) | async-done | bytes 393248 | tf_op jit(solution)/shard_map/all_to_all | solution.py:225
  190.8 3.5 all-to-all-start
  197.9 4.7 convolution_convert_fusion.5
  204.3 18.1 %all-to-all-done = bf16[1,256,3,12,64]{1,4,2,0,3:T(8,128)(2,1)S(1)} async-done(((bf16[1,256,3,12,64]{1,4,2,0,3:T(8,128)(2,1)}), bf16[1,256,3,12,64]{1,4,2,0,3:T(8,128)(2,1)S(1)}, u32[]{:S(2)}, u32[]{:S(2)}) %all-to-all-start) | async-done | bytes 1179680 | tf_op jit(solution)/shard_map/all_to_all | solution.py:148
  224.3 2.8 all_to_all.56
  230.5 2.9 fusion.5
  233.3 4.5 multiply_reduce_fusion
  241.9 4.5 multiply_reduce_fusion.1
  246.3 9.2 %multiply_convert_fusion = (bf16[3,512,1024]{2,1,0:T(8,128)(2,1)S(1)}, bf16[3,512,1024]{2,1,0:T(8,128)(2,1)S(1)}) fusion(f32[3,512,1024]{2,1,0:T(8,128)} %get-tuple-element.99, f32[3,512]{1,0:T(4,128)S(1)} %get-tuple-element.98, f32[3,512]{1,0:T(4,128)S(1)} %log_add_fusion, f32[3,512,1024]{2,1,0:T(8,128)S(1)} %get-tuple-element.93, ...), kind=kLoop, calls=%fused_computation | loop fusion | flops 22020096 | bytes 32530432 | tf_op jit(solution)/shard_map/convert_element_type | solution.py:243
  258.6 2.0 fusion.33
  263.5 4.6 copy.62
  268.2 3.1 reshape.771
  271.3 4.4 all-to-all-start.4
  275.7 5.4 %fusion.41 = bf16[1,512,3,64]{1,3,2,0:T(8,128)(2,1)S(1)} fusion(f32[3,512,1024]{2,1,0:T(8,128)} %copy-done, f32[3,512]{1,0:T(4,128)} %copy-done.31, f32[3,512]{1,0:T(4,128)} %copy-done.30, pred[512,1024]{1,0:T(8,128)(4,1)} %copy-done.9, bf16[1,1024,3,3,64]{1,4,3,2,0:T(8,128)(2,1)} %copy-done.10), kind=kOutput, calls=%fused_computation.84 | convolution fusion | flops 209289216 | bytes 7421952 | tf_op jit(solution)/shard_map/shqk,skhe->sqhe/dot_general | solution.py:183
  281.2 3.0 fusion.40
  286.4 17.8 %all-to-all-done.4 = bf16[4,2,73728]{2,1,0:T(2,128)(2,1)} async-done(((bf16[4,2,73728]{2,1,0:T(2,128)(2,1)}), bf16[4,2,73728]{2,1,0:T(2,128)(2,1)}, u32[]{:S(2)}, u32[]{:S(2)}) %all-to-all-start.4) | async-done | bytes 1179680 | tf_op jit(solution)/shard_map/all_to_all | solution.py:70
  304.2 4.1 all-to-all-start.2
  308.4 3.6 reshape.772
  312.0 3.7 copy.63
  320.7 2.9 fusion.62
  324.6 3.1 constant_dynamic-slice_fusion
  334.3 2.8 pad_maximum_fusion
  340.6 2.3 fusion.31
  347.0 2.8 reduce-scatter.13.cloned.1.call-done
  350.6 17.0 %all-reduce.7 = (bf16[5,192]{1,0:T(8,128)(2,1)S(1)}, bf16[768]{0:T(1024)(128)(2,1)S(1)}) all-reduce(bf16[5,192]{1,0:T(8,128)(2,1)S(1)} %copy.70, bf16[768]{0:T(1024)(128)(2,1)} %dynamic-slice.8), channel_id=1, replica_groups=mesh['fsdp'=4,'ctx'=4,'tensor'=2] {'ctx','tensor'}, use_global_device_ids=true, to_apply=%region_24.25 | all-reduce | flops 1728 | bytes 6912 | tf_op jit(solution)/shard_map/psum | solution.py:310
  368.8 40.1 %all-reduce.16.cloned.1.call-done = bf16[1536,2,192]{0,1,2:T(2,128)(2,1)} async-done(((bf16[1536,2,192]{0,1,2:T(2,128)(2,1)}), bf16[1536,2,192]{0,1,2:T(2,128)(2,1)}) %all-reduce.16.cloned.1.call-update) | async-done | bytes 1179664 | tf_op jit(solution)/shard_map/psum | solution.py:313
  408.9 3.7 fusion.102
  412.6 55.6 %reduce-scatter.11.cloned.1.call-done = bf16[192,3072]{1,0:T(8,128)(2,1)} async-done(((bf16[768,3072]{1,0:T(8,128)(2,1)}), bf16[192,3072]{1,0:T(8,128)(2,1)}) %reduce-scatter.11.cloned.1.call-update) | async-done | bytes 1179664 | tf_op jit(solution)/shard_map/reduce_scatter | solution.py:282
  469.7 60.6 %all-reduce.14.cloned.1.call-done = bf16[192,3072]{1,0:T(8,128)(2,1)} async-done(((bf16[192,3072]{1,0:T(8,128)(2,1)}), bf16[192,3072]{1,0:T(8,128)(2,1)}) %all-reduce.14.cloned.1.call-update) | async-done | bytes 1179664 | tf_op jit(solution)/shard_map/psum | solution.py:309
  532.1 2.5 slice.144
  (230 shorter events, 64.5 us)
Async XLA Ops:
  7.2 27.3 %copy-start.3 = (bf16[1,256,768]{2,1,0:T(8,128)(2,1)S(1)}, bf16[1,256,768]{2,1,0:T(8,128)(2,1)}, u32[]{:S(2)}) copy-start(bf16[1,256,768]{2,1,0:T(8,128)(2,1)} %param.14) | copy-start | bytes 1179652
  7.2 30.2 %copy-start.5 = (bf16[1,256,768]{2,1,0:T(8,128)(2,1)S(1)}, bf16[1,256,768]{2,1,0:T(8,128)(2,1)}, u32[]{:S(2)}) copy-start(bf16[1,256,768]{2,1,0:T(8,128)(2,1)} %param.15) | copy-start | bytes 1179652
  7.2 42.8 %all-gather.10.cloned.1.call-start = ((), (), s32[]{:S(2)}) async-start(), calls=%async_computation.11 | async-start | bytes 2949120 | tf_op jit(solution)/shard_map/all_gather | solution.py:114
  7.9 81.3 %all-gather.12.cloned.1.call-start = ((), (), s32[]{:S(2)}) async-start(), calls=%async_computation.12 | async-start | bytes 2949120 | tf_op jit(solution)/shard_map/all_gather | solution.py:115
  8.7 117.2 %all-gather.8.cloned.1.call-start = ((), (), s32[]{:S(2)}) async-start(), calls=%async_computation.10 | async-start | bytes 1474560 | tf_op jit(solution)/shard_map/all_gather | solution.py:113
  9.4 158.2 %all-gather.6.cloned.1.call-start = ((), (), s32[]{:S(2)}) async-start(), calls=%async_computation.9 | async-start | bytes 4423680 | tf_op jit(solution)/shard_map/all_gather | solution.py:112
  10.0 192.6 %reduce-scatter.9.cloned.1.call-start = ((), (), s32[]{:S(2)}) async-start(), calls=%async_computation.14 | async-start | bytes 1179648 | tf_op jit(solution)/shard_map/reduce_scatter | solution.py:74
  26.0 9.0 %copy-start.24 = (f32[768]{0:T(1024)}, f32[768]{0:T(1024)S(1)}, u32[]{:S(2)}) copy-start(f32[768]{0:T(1024)S(1)} %convert_element_type.220) | copy-start | bytes 9220
  34.4 2.9 copy-start.21
  89.2 5.9 %copy-start.39 = (bf16[768,1536]{1,0:T(8,128)(2,1)S(1)}, bf16[768,1536]{1,0:T(8,128)(2,1)}, u32[]{:S(2)}) copy-start(bf16[768,1536]{1,0:T(8,128)(2,1)} %all-gather.10.cloned.1.call-done) | copy-start | bytes 7077892
  97.4 227.2 %all-reduce.18.cloned.1.call-start = ((), (), s32[]{:S(2)}) async-start(), calls=%async_computation.19 | async-start | bytes 9437184
  97.5 3.0 copy-start.44
  117.2 7.2 %copy-start.38 = (s32[1,256]{1,0:T(1,128)S(1)}, s32[1,256]{1,0:T(1,128)}, u32[]{:S(2)}) copy-start(s32[1,256]{1,0:T(1,128)} %param.17) | copy-start | bytes 3076
  117.2 7.2 %copy-start.41 = (bf16[192]{0:T(256)(128)(2,1)S(1)}, bf16[192]{0:T(256)(128)(2,1)}, u32[]{:S(2)}) copy-start(bf16[192]{0:T(256)(128)(2,1)} %param.22) | copy-start | bytes 1156
  117.2 7.5 %copy-start.42 = (bf16[192]{0:T(256)(128)(2,1)S(1)}, bf16[192]{0:T(256)(128)(2,1)}, u32[]{:S(2)}) copy-start(bf16[192]{0:T(256)(128)(2,1)} %param.23) | copy-start | bytes 1156
  117.2 7.7 %copy-start.43 = (bf16[192]{0:T(256)(128)(2,1)S(1)}, bf16[192]{0:T(256)(128)(2,1)}, u32[]{:S(2)}) copy-start(bf16[192]{0:T(256)(128)(2,1)} %param.26) | copy-start | bytes 1156
  119.7 55.0 %all-to-all-start.1 = ((bf16[4,2,128]{2,1,0:T(2,128)(2,1)}), bf16[4,2,128]{2,1,0:T(2,128)(2,1)}, u32[]{:S(2)}, u32[]{:S(2)}) async-start(bf16[4,2,128]{2,1,0:T(2,128)(2,1)} %reshape.767), calls=%async_computation.1 | async-start | bytes 4096 | tf_op jit(solution)/shard_map/all_to_all | solution.py:149
  174.4 4.8 copy-start.19
  174.7 16.1 %all-to-all-start.3 = ((bf16[1,256,1,12,64]{1,4,2,0,3:T(8,128)(2,1)}), bf16[1,256,1,12,64]{1,4,2,0,3:T(8,128)(2,1)S(1)}, u32[]{:S(2)}, u32[]{:S(2)}) async-start(bf16[1,256,1,12,64]{1,4,2,0,3:T(8,128)(2,1)} %bitcast.40), calls=%async_computation.4 | async-start | bytes 786432 | tf_op jit(solution)/shard_map/all_to_all | solution.py:225
  179.4 15.0 %copy-start.6 = (bf16[1,256,768]{2,1,0:T(8,128)(2,1)S(1)}, bf16[1,256,768]{2,1,0:T(8,128)(2,1)}, u32[]{:S(2)}) copy-start(bf16[1,256,768]{2,1,0:T(8,128)(2,1)} %param.15) | copy-start | bytes 1179652
  190.8 31.6 %all-to-all-start = ((bf16[1,256,3,12,64]{1,4,2,0,3:T(8,128)(2,1)}), bf16[1,256,3,12,64]{1,4,2,0,3:T(8,128)(2,1)S(1)}, u32[]{:S(2)}, u32[]{:S(2)}) async-start(bf16[1,256,3,12,64]{1,4,2,0,3:T(8,128)(2,1)} %copy.54), calls=%async_computation | async-start | bytes 2359296 | tf_op jit(solution)/shard_map/all_to_all | solution.py:148
  194.3 146.2 %reduce-scatter.7.cloned.1.call-start = ((), (), s32[]{:S(2)}) async-start(), calls=%async_computation.13 | async-start | bytes 1179648 | tf_op jit(solution)/shard_map/reduce_scatter | solution.py:74
  197.3 49.1 %copy-start.9 = (pred[512,1024]{1,0:T(8,128)(4,1)}, pred[512,1024]{1,0:T(8,128)(4,1)S(1)}, u32[]{:S(2)}) copy-start(pred[512,1024]{1,0:T(8,128)(4,1)S(1)} %get-tuple-element.86) | copy-start | bytes 1572868
  197.3 60.0 %copy-start.7 = (pred[512,1024]{1,0:T(8,128)(4,1)}, pred[512,1024]{1,0:T(8,128)(4,1)S(1)}, u32[]{:S(2)}) copy-start(pred[512,1024]{1,0:T(8,128)(4,1)S(1)} %get-tuple-element.85) | copy-start | bytes 1572868
  197.9 43.2 %copy-start.17 = (bf16[1,1024,3,64]{1,3,2,0:T(8,128)(2,1)}, bf16[1,1024,3,64]{1,3,2,0:T(8,128)(2,1)S(1)}, u32[]{:S(2)}) copy-start(bf16[1,1024,3,64]{1,3,2,0:T(8,128)(2,1)S(1)} %squeeze.45) | copy-start | bytes 1179652
  227.1 33.4 %copy-start.10 = (bf16[1,1024,3,3,64]{1,4,3,2,0:T(8,128)(2,1)}, bf16[1,1024,3,3,64]{1,4,3,2,0:T(8,128)(2,1)S(1)}, u32[]{:S(2)}) copy-start(bf16[1,1024,3,3,64]{1,4,3,2,0:T(8,128)(2,1)S(1)} %all_to_all.56) | copy-start | bytes 3538948
  228.6 17.8 %copy-start = (f32[3,512,1024]{2,1,0:T(8,128)}, f32[3,512,1024]{2,1,0:T(8,128)S(1)}, u32[]{:S(2)}) copy-start(f32[3,512,1024]{2,1,0:T(8,128)S(1)} %get-tuple-element.93) | copy-start | bytes 18874372
  241.0 5.3 copy-start.34
  255.5 3.0 copy-start.46
  271.3 9.9 %slice-start = ((s8[6291456]{0:T(1024)(128)(4,1)}), s8[2097152]{0:T(1024)(128)(4,1)S(1)}, s32[]{:S(2)}) async-start(s8[6291456]{0:T(1024)(128)(4,1)} %bitcast.274), calls=%async_computation.20 | async-start | bytes 4194304
  271.3 32.9 %all-to-all-start.4 = ((bf16[4,2,73728]{2,1,0:T(2,128)(2,1)}), bf16[4,2,73728]{2,1,0:T(2,128)(2,1)}, u32[]{:S(2)}, u32[]{:S(2)}) async-start(bf16[4,2,73728]{2,1,0:T(2,128)(2,1)} %reshape.771), calls=%async_computation.5 | async-start | bytes 2359296 | tf_op jit(solution)/shard_map/all_to_all | solution.py:70
  275.7 5.5 %slice-start.1 = ((s8[6291456]{0:T(1024)(128)(4,1)}), s8[4194304]{0:T(1024)(128)(4,1)S(1)}, s32[]{:S(2)}) async-start(s8[6291456]{0:T(1024)(128)(4,1)} %bitcast.274), calls=%async_computation.21 | async-start | bytes 8388608
  275.7 5.5 %copy-start.8 = (pred[512,1024]{1,0:T(8,128)(4,1)S(1)}, pred[512,1024]{1,0:T(8,128)(4,1)}, u32[]{:S(2)}) copy-start(pred[512,1024]{1,0:T(8,128)(4,1)} %copy-done.7) | copy-start | bytes 1572868
  275.7 5.5 %copy-start.33 = (f32[3,512]{1,0:T(4,128)S(1)}, f32[3,512]{1,0:T(4,128)}, u32[]{:S(2)}) copy-start(f32[3,512]{1,0:T(4,128)} %copy-done.32) | copy-start | bytes 18436
  275.7 5.5 %copy-start.35 = (f32[3,512]{1,0:T(4,128)S(1)}, f32[3,512]{1,0:T(4,128)}, u32[]{:S(2)}) copy-start(f32[3,512]{1,0:T(4,128)} %copy-done.34) | copy-start | bytes 18436
  304.2 23.6 %all-to-all-start.2 = ((bf16[4,2,24576]{2,1,0:T(2,128)(2,1)}), bf16[4,2,24576]{2,1,0:T(2,128)(2,1)}, u32[]{:S(2)}, u32[]{:S(2)}) async-start(bf16[4,2,24576]{2,1,0:T(2,128)(2,1)} %reshape.769), calls=%async_computation.2 | async-start | bytes 786432 | tf_op jit(solution)/shard_map/all_to_all | solution.py:70
  308.3 41.4 %reduce-scatter.13.cloned.1.call-start = ((), (), s32[]{:S(2)}) async-start(), calls=%async_computation.18 | async-start | bytes 245760
  320.7 2.9 copy-start.36
  320.7 2.9 copy-start.37
  324.5 84.3 %all-reduce.16.cloned.1.call-start = ((), (), s32[]{:S(2)}) async-start(), calls=%async_computation.17 | async-start | bytes 2359296 | tf_op jit(solution)/shard_map/psum | solution.py:313
  327.7 5.3 copy-start.23
  327.7 5.3 copy-start.29
  327.7 140.4 %reduce-scatter.11.cloned.1.call-start = ((), (), s32[]{:S(2)}) async-start(), calls=%async_computation.15 | async-start | bytes 5898240 | tf_op jit(solution)/shard_map/reduce_scatter | solution.py:282
  337.1 3.5 copy-start.14
  337.1 3.5 copy-start.15
  337.1 8.5 %copy-start.16 = (f32[256,768]{1,0:T(8,128)S(1)}, f32[256,768]{1,0:T(8,128)}, u32[]{:S(2)}) copy-start(f32[256,768]{1,0:T(8,128)} %get-tuple-element.100) | copy-start | bytes 2359300
  337.1 8.5 %copy-start.26 = (f32[768]{0:T(1024)S(1)}, f32[768]{0:T(1024)}, u32[]{:S(2)}) copy-start(f32[768]{0:T(1024)} %copy-done.24) | copy-start | bytes 9220
  337.1 193.2 %all-reduce.14.cloned.1.call-start = ((), (), s32[]{:S(2)}) async-start(), calls=%async_computation.16 | async-start | bytes 2359296 | tf_op jit(solution)/shard_map/psum | solution.py:309
  (17 other events, 35.7 us)
Sparse Core Ops, SparseCore 0:
  9.8 40.0 all-gather.9
  51.8 37.3 all-gather.11
  91.0 27.5 all-gather.7
  120.4 47.2 all-gather.5
  170.3 8.1 reduce-scatter.8
  181.6 113.3 all-reduce.17
  297.9 8.1 reduce-scatter.6
  324.6 25.0 reduce-scatter.12
  352.7 56.1 all-reduce.15
  411.7 56.3 reduce-scatter.10
  470.5 59.7 all-reduce.13
where the time goes:
time: 552 us; the launch traced here: 541 us
  waiting for transfers between devices  269 us (49%)
  local copies, waits for them, and re-layouts  78.2 us (14%)
  matrix products  67.9 us (12%)
  blocking collectives  56.5 us (10%)
  other arithmetic  30.6 us (6%)
  starting transfers between devices  21.8 us (4%)
  between operations  17.2 us (3%)
    psum x1, waiting for transfers between devices, shards(): lax.psum(attn_grad, ('ctx', 'tensor')).astype(jnp.float32)  60.6 us
    reduce_scatter x1, waiting for transfers between devices, shards(): lax.psum_scatter(jnp.concatenate([qkv_part, proj_part], axis=1).astype(jn...  55.6 us
    psum x1, waiting for transfers between devices, shards(): ffn_sum = lax.psum(ffn_part.astype(jnp.bfloat16), 'ctx').astype(jnp.float32)  40.1 us
    unnamed x126, local copies, waits for them, and re-layouts  29.1 us
    all_gather x1, waiting for transfers between devices, shards(): lax.all_gather(down_matrix, 'fsdp', axis=1, tiled=True)  28.2 us
    unnamed x2, blocking collectives  27.5 us
    all_gather x1, waiting for transfers between devices, shards(): lax.all_gather(query_key_value_weight, 'fsdp', axis=0, tiled=True)  22.7 us
    all_to_all x1, waiting for transfers between devices, shards(): lax.all_to_all(packed, 'ctx', split_axis=3, concat_axis=1, tiled=True)  18.1 us
  transfers between devices with their start and end apart: 16, of which 10 were waited for; matrix products, arithmetic and copies ran while one was open for 30% of the time, Pallas kernels for 0%

commit v1 on v0

--- a/solution.py
+++ b/solution.py
@@ -310,7 +310,11 @@
         lax.psum(small_part.astype(jnp.bfloat16), ("ctx", "tensor")).astype(jnp.float32),
         lax.psum(bias_part.astype(jnp.bfloat16), ("ctx", "tensor")).astype(jnp.float32),
     )
-    ffn_sum = lax.psum(ffn_part.astype(jnp.bfloat16), "ctx").astype(jnp.float32)
+
+    def choose_the_orders(array_in, a_name):
+        return lax.all_gather(array_in, axis_name=a_name).sum(axis=0)
+
+    ffn_sum = choose_the_orders(ffn_part.astype(jnp.bfloat16), "ctx").astype(jnp.float32)
     return (
         layer_output,
         input_grad.reshape(seq_count, piece_len, model_width),

time: 552 us -> 609 us (1.10)
  waiting for transfers between devices: 269 us -> 290 us
  blocking collectives: 56.5 us -> 70.9 us
  local copies, waits for them, and re-layouts: 78.2 us -> 89.3 us
  other arithmetic: 30.6 us -> 39.6 us
    all_gather x0 -> x1, waiting for transfers between devices: none -> 62.3 us  [choose_the_orders(): return lax.all_gather(array_in, axis_name=a_name).sum(axis=0)]
    psum x1 -> x0, waiting for transfers between devices: 40.1 us -> none  [shards(): ffn_sum = lax.psum(ffn_part.astype(jnp.bfloat16), 'ctx').astype(jnp.float32)]
    all_to_all x1, waiting for transfers between devices: 18.1 us -> 0.5 us  [shards(): lax.all_to_all(packed, 'ctx', split_axis=3, concat_axis=1, tiled=True)]
    reduce_scatter x1, waiting for transfers between devices: 55.6 us -> 38.8 us  [shards(): lax.psum_scatter(jnp.concatenate([qkv_part, proj_part], axis=1).astype(jn...]
    all_to_all x0 -> x1, blocking collectives: none -> 16.5 us  [to_tokens(): lax.all_to_all(blocks, 'ctx', split_axis=1, concat_axis=3, tiled=True)]
    unnamed x13, waiting for transfers between devices: 5.47 us -> 21.9 us
    all_gather x1, waiting for transfers between devices: 10.2 us -> 25.7 us  [shards(): lax.all_gather(up_matrix, 'fsdp', axis=0, tiled=True)]
    all_gather x0 -> x1, local copies, waits for them, and re-layouts: none -> 12 us  [choose_the_orders(): return lax.all_gather(array_in, axis_name=a_name).sum(axis=0)]
  transfers between devices with their start and end apart: 16 -> 15, of which waited for: 10 -> 10; matrix products, arithmetic and copies ran while one was open for 30% -> 32% of each run, Pallas kernels for 0% -> 0%
where the time goes in v1:
time: 609 us; the launch traced here: 598 us
  waiting for transfers between devices  290 us (48%)
  local copies, waits for them, and re-layouts  89.3 us (15%)
  matrix products  71.6 us (12%)
  blocking collectives  70.9 us (12%)
  other arithmetic  39.6 us (7%)
  starting transfers between devices  19.9 us (3%)
  between operations  17.2 us (3%)
    all_gather x1, waiting for transfers between devices, choose_the_orders(): return lax.all_gather(array_in, axis_name=a_name).sum(axis=0)  62.3 us
    psum x1, waiting for transfers between devices, shards(): lax.psum(attn_grad, ('ctx', 'tensor')).astype(jnp.float32)  55.9 us
    reduce_scatter x1, waiting for transfers between devices, shards(): lax.psum_scatter(jnp.concatenate([qkv_part, proj_part], axis=1).astype(jn...  38.8 us
    unnamed x127, local copies, waits for them, and re-layouts  31.9 us
    all_gather x1, waiting for transfers between devices, shards(): lax.all_gather(down_matrix, 'fsdp', axis=1, tiled=True)  28.3 us
    unnamed x2, blocking collectives  26.2 us
    all_gather x1, waiting for transfers between devices, shards(): lax.all_gather(up_matrix, 'fsdp', axis=0, tiled=True)  25.7 us
    all_gather x1, waiting for transfers between devices, shards(): lax.all_gather(query_key_value_weight, 'fsdp', axis=0, tiled=True)  25.6 us
  transfers between devices with their start and end apart: 15, of which 10 were waited for; matrix products, arithmetic and copies ran while one was open for 32% of the time, Pallas kernels for 0%

profile of v1, /device:TPU:0, one launch (start us, length us, event | category | flops | bytes accessed | tf_op | source)
XLA Modules:
  0.0 598.0 jit_solution(12744581481940037379)
XLA Ops:
  12.5 6.3 %all-to-all-start.1 = ((bf16[4,2,128]{2,1,0:T(2,128)(2,1)}), bf16[4,2,128]{2,1,0:T(2,128)(2,1)}, u32[]{:S(2)}, u32[]{:S(2)}) async-start(bf16[4,2,128]{2,1,0:T(2,128)(2,1)} %reshape.768), calls=%async_computation.1 | async-start | bytes 4096 | tf_op jit(solution)/shard_map/all_to_all | solution.py:149
  23.2 9.9 %all-reduce.9 = (bf16[768]{0:T(1024)(128)(2,1)S(1)}, bf16[768]{0:T(1024)(128)(2,1)S(1)}) all-reduce(bf16[768]{0:T(1024)(128)(2,1)S(1)} %dynamic-update-slice.2, bf16[768]{0:T(1024)(128)(2,1)S(1)} %dynamic-update-slice.3), channel_id=1, replica_groups=mesh['fsdp'=4,'ctx'=4,'tensor'=2] {'fsdp'}, use_global_device_ids=true, to_apply=%add.2 | all-reduce | flops 1536 | bytes 6144
  33.8 7.4 %all-gather.1 = bf16[4,1,768]{2,1,0:T(2,128)(2,1)S(1)} all-gather(bf16[1,1,768]{2,1,0:T(2,128)(2,1)S(1)} %reshape.747), channel_id=1, replica_groups=mesh['fsdp'=4,'ctx'=4,'tensor'=2] {'fsdp'}, dimensions={0}, use_global_device_ids=true | all-gather | bytes 7680 | tf_op jit(solution)/shard_map/all_gather | solution.py:121
  45.5 2.4 all_gather.48
  47.9 2.4 all_gather.53
  53.8 25.7 %all-gather.12.cloned.1.call-done = bf16[768,1536]{1,0:T(8,128)(2,1)} async-done(((bf16[192,1536]{1,0:T(8,128)(2,1)}), bf16[768,1536]{1,0:T(8,128)(2,1)}) %all-gather.12.cloned.1.call-update) | async-done | bytes 2359312 | tf_op jit(solution)/shard_map/all_gather | solution.py:114
  79.5 11.0 %multiply_convert_fusion.2 = (bf16[512,1536]{1,0:T(8,128)(2,1)}, f32[512,1536]{1,0:T(8,128)}, f32[512,1536]{1,0:T(8,128)}) fusion(f32[1536]{0:T(1024)S(1)} %dynamic_slice.29, bf16[512,768]{1,0:T(8,128)(2,1)S(1)} %bitcast.298, bf16[768,1536]{1,0:T(8,128)(2,1)} %all-gather.12.cloned.1.call-done), kind=kOutput, calls=%fused_computation.30 | convolution fusion | flops 1259864064 | bytes 11016192 | tf_op jit(solution)/shard_map/dot_general | solution.py:201
  90.4 28.3 %all-gather.14.cloned.1.call-done = bf16[1536,768]{0,1:T(8,128)(2,1)} async-done(((bf16[1536,192]{0,1:T(8,128)(2,1)}), bf16[1536,768]{0,1:T(8,128)(2,1)}) %all-gather.14.cloned.1.call-update) | async-done | bytes 2359312 | tf_op jit(solution)/shard_map/all_gather | solution.py:115
  118.7 6.9 %convert_reduce_fusion = (bf16[1536]{0:T(1024)(128)(2,1)S(1)}, bf16[512,1536]{1,0:T(8,128)(2,1)}) fusion(f32[512,1536]{1,0:T(8,128)} %get-tuple-element.57, f32[512,1536]{1,0:T(8,128)} %get-tuple-element.91, bf16[512,768]{1,0:T(8,128)(2,1)S(1)} %bitcast.296, bf16[1536,768]{0,1:T(8,128)(2,1)} %all-gather.14.cloned.1.call-done), kind=kOutput, calls=%fused_computation.24 | convolution fusion | flops 1220540928 | bytes 11013120 | tf_op jit(solution)/shard_map/td,fd->tf/dot_general | solution.py:208
  125.8 16.3 %all-reduce.8 = (bf16[768]{0:T(1024)(128)(2,1)S(1)}, bf16[768]{0:T(1024)(128)(2,1)S(1)}, bf16[3072]{0:T(1024)(128)(2,1)}, bf16[768]{0:T(1024)(128)(2,1)}) all-reduce(bf16[768]{0:T(1024)(128)(2,1)S(1)} %dynamic-update-slice.1, bf16[768]{0:T(1024)(128)(2,1)S(1)} %dynamic-update-slice, ...), channel_id=1, replica_groups=mesh['fsdp'=4,'ctx'=4,'tensor'=2] {'fsdp'}, use_global_device_ids=true, to_apply=%add.1 | all-reduce | flops 5376 | bytes 21504
  142.1 25.6 %all-gather.8.cloned.1.call-done = bf16[768,2304]{1,0:T(8,128)(2,1)} async-done(((bf16[192,2304]{1,0:T(8,128)(2,1)}), bf16[768,2304]{1,0:T(8,128)(2,1)}) %all-gather.8.cloned.1.call-update) | async-done | bytes 3538960 | tf_op jit(solution)/shard_map/all_gather | solution.py:112
  167.7 4.5 copy.52
  172.3 2.3 fusion.73
  174.8 4.6 all-to-all-start.3
  180.7 10.1 %all-to-all-done.3 = bf16[1,256,1,12,64]{1,4,2,0,3:T(8,128)(2,1)S(1)} async-done(((bf16[1,256,1,12,64]{1,4,2,0,3:T(8,128)(2,1)}), bf16[1,256,1,12,64]{1,4,2,0,3:T(8,128)(2,1)S(1)}, u32[]{:S(2)}, u32[]{:S(2)}) %all-to-all-start.3) | async-done | bytes 393248 | tf_op jit(solution)/shard_map/all_to_all | solution.py:225
  190.9 3.5 all-to-all-start
  194.8 4.5 convolution_convert_fusion.4
  202.2 3.2 fusion.16
  206.8 2.5 pad_maximum_fusion.1
  209.4 12.6 %copy.64 = bf16[1536,2,768]{0,1,2:T(2,128)(2,1)} copy(bf16[1536,2,768]{2,0,1:T(8,128)(2,1)} %pad_maximum_fusion.1) | data formatting | bytes 9437184 | tf_op jit(solution)/shard_map/stack | solution.py:216
  230.8 4.6 multiply_reduce_fusion
  235.4 4.5 multiply_reduce_fusion.1
  239.9 9.2 %multiply_convert_fusion = (bf16[3,512,1024]{2,1,0:T(8,128)(2,1)S(1)}, bf16[3,512,1024]{2,1,0:T(8,128)(2,1)S(1)}) fusion(f32[3,512,1024]{2,1,0:T(8,128)} %get-tuple-element.99, f32[3,512]{1,0:T(4,128)S(1)} %get-tuple-element.98, f32[3,512]{1,0:T(4,128)S(1)} %log_add_fusion, f32[3,512,1024]{2,1,0:T(8,128)S(1)} %get-tuple-element.93, ...), kind=kLoop, calls=%fused_computation | loop fusion | flops 22020096 | bytes 32530432 | tf_op jit(solution)/shard_map/convert_element_type | solution.py:243
  252.8 2.0 fusion.5
  255.2 1.9 fusion.33
  258.3 4.7 copy.61
  263.0 3.1 reshape.772
  266.1 4.5 all-to-all-start.4
  270.5 4.5 convolution_convert_fusion.5
  278.1 20.3 %all-to-all-done.4 = bf16[4,2,73728]{2,1,0:T(2,128)(2,1)} async-done(((bf16[4,2,73728]{2,1,0:T(2,128)(2,1)}), bf16[4,2,73728]{2,1,0:T(2,128)(2,1)}, u32[]{:S(2)}, u32[]{:S(2)}) %all-to-all-start.4) | async-done | bytes 1179680 | tf_op jit(solution)/shard_map/all_to_all | solution.py:70
  298.4 3.5 reshape.773
  301.9 3.8 copy.62
  311.4 2.9 fusion.62
  315.6 19.2 %all-reduce.15.cloned.1.call-done = bf16[1536,2,768]{0,1,2:T(2,128)(2,1)} async-done(((bf16[1536,2,768]{0,1,2:T(2,128)(2,1)}), bf16[1536,2,768]{0,1,2:T(2,128)(2,1)}) %all-reduce.15.cloned.1.call-update) | async-done | bytes 4718608
  334.8 3.1 constant_dynamic-slice_fusion
  338.1 4.8 fusion.41
  343.0 4.9 fusion.40
  350.1 16.5 %all_to_all.72 = bf16[4,2,24576]{2,1,0:T(2,128)(2,1)} all-to-all(bf16[4,2,24576]{2,1,0:T(2,128)(2,1)} %reshape.770), channel_id=1, replica_groups=mesh['fsdp'=4,'ctx'=4,'tensor'=2] {'ctx'}, dimensions={0} | all-to-all | bytes 786432 | tf_op jit(solution)/shard_map/all_to_all | solution.py:70
  373.0 2.9 pad_maximum_fusion
  379.3 2.3 fusion.31
  386.6 16.1 %all-reduce.7 = (bf16[5,192]{1,0:T(8,128)(2,1)S(1)}, bf16[768]{0:T(1024)(128)(2,1)S(1)}) all-reduce(bf16[5,192]{1,0:T(8,128)(2,1)S(1)} %copy.73, bf16[768]{0:T(1024)(128)(2,1)} %dynamic-slice.8), channel_id=1, replica_groups=mesh['fsdp'=4,'ctx'=4,'tensor'=2] {'ctx','tensor'}, use_global_device_ids=true, to_apply=%region_24.25 | all-reduce | flops 1728 | bytes 6912 | tf_op jit(solution)/shard_map/psum | solution.py:310
  403.9 62.3 %all-gather.16.cloned.1.call-done = bf16[6144,2,192]{0,1,2:T(2,128)(2,1)} async-done(((bf16[1536,2,192]{0,1,2:T(2,128)(2,1)}), bf16[6144,2,192]{0,1,2:T(2,128)(2,1)}) %all-gather.16.cloned.1.call-update) | async-done | bytes 4718608 | tf_op jit(solution)/shard_map/all_gather | solution.py:315
  466.2 12.0 %copy.71 = bf16[6144,2,192]{2,0,1:T(8,128)(2,1)} copy(bf16[6144,2,192]{0,1,2:T(2,128)(2,1)} %all-gather.16.cloned.1.call-done) | data formatting | bytes 9437184 | tf_op jit(solution)/shard_map/all_gather | solution.py:315
  478.3 5.6 reduce_sum.166
  485.6 38.8 %reduce-scatter.11.cloned.1.call-done = bf16[192,3072]{1,0:T(8,128)(2,1)} async-done(((bf16[768,3072]{1,0:T(8,128)(2,1)}), bf16[192,3072]{1,0:T(8,128)(2,1)}) %reduce-scatter.11.cloned.1.call-update) | async-done | bytes 1179664 | tf_op jit(solution)/shard_map/reduce_scatter | solution.py:282
  526.4 3.0 copy.67
  530.9 55.9 %all-reduce.13.cloned.1.call-done = bf16[192,3072]{1,0:T(8,128)(2,1)} async-done(((bf16[192,3072]{1,0:T(8,128)(2,1)}), bf16[192,3072]{1,0:T(8,128)(2,1)}) %all-reduce.13.cloned.1.call-update) | async-done | bytes 1179664 | tf_op jit(solution)/shard_map/psum | solution.py:309
  588.6 2.5 slice.144
  (233 shorter events, 71.4 us)
Async XLA Ops:
  7.2 37.8 %copy-start.2 = (bf16[1,256,768]{2,1,0:T(8,128)(2,1)S(1)}, bf16[1,256,768]{2,1,0:T(8,128)(2,1)}, u32[]{:S(2)}) copy-start(bf16[1,256,768]{2,1,0:T(8,128)(2,1)} %param.14) | copy-start | bytes 1179652
  7.2 40.7 %copy-start.4 = (bf16[1,256,768]{2,1,0:T(8,128)(2,1)S(1)}, bf16[1,256,768]{2,1,0:T(8,128)(2,1)}, u32[]{:S(2)}) copy-start(bf16[1,256,768]{2,1,0:T(8,128)(2,1)} %param.15) | copy-start | bytes 1179652
  7.2 43.9 %all-gather.10.cloned.1.call-start = ((), (), s32[]{:S(2)}) async-start(), calls=%async_computation.10 | async-start | bytes 1474560 | tf_op jit(solution)/shard_map/all_gather | solution.py:113
  7.9 71.5 %all-gather.12.cloned.1.call-start = ((), (), s32[]{:S(2)}) async-start(), calls=%async_computation.11 | async-start | bytes 2949120 | tf_op jit(solution)/shard_map/all_gather | solution.py:114
  8.7 110.0 %all-gather.14.cloned.1.call-start = ((), (), s32[]{:S(2)}) async-start(), calls=%async_computation.12 | async-start | bytes 2949120 | tf_op jit(solution)/shard_map/all_gather | solution.py:115
  9.4 158.3 %all-gather.8.cloned.1.call-start = ((), (), s32[]{:S(2)}) async-start(), calls=%async_computation.9 | async-start | bytes 4423680 | tf_op jit(solution)/shard_map/all_gather | solution.py:112
  12.5 162.3 %all-to-all-start.1 = ((bf16[4,2,128]{2,1,0:T(2,128)(2,1)}), bf16[4,2,128]{2,1,0:T(2,128)(2,1)}, u32[]{:S(2)}, u32[]{:S(2)}) async-start(bf16[4,2,128]{2,1,0:T(2,128)(2,1)} %reshape.768), calls=%async_computation.1 | async-start | bytes 4096 | tf_op jit(solution)/shard_map/all_to_all | solution.py:149
  33.1 12.4 %copy-start.30 = (f32[768]{0:T(1024)}, f32[768]{0:T(1024)S(1)}, u32[]{:S(2)}) copy-start(f32[768]{0:T(1024)S(1)} %convert_element_type.222) | copy-start | bytes 9220
  45.0 5.3 copy-start.27
  45.2 5.0 copy-start.33
  47.9 42.6 %copy-start.22 = (bf16[2,256,768]{2,1,0:T(8,128)(2,1)}, bf16[2,256,768]{2,1,0:T(8,128)(2,1)S(1)}, u32[]{:S(2)}) copy-start(bf16[2,256,768]{2,1,0:T(8,128)(2,1)S(1)} %all_gather.48) | copy-start | bytes 2359300
  50.2 68.5 %copy-start.20 = (bf16[2,256,768]{2,1,0:T(8,128)(2,1)}, bf16[2,256,768]{2,1,0:T(8,128)(2,1)S(1)}, u32[]{:S(2)}) copy-start(bf16[2,256,768]{2,1,0:T(8,128)(2,1)S(1)} %all_gather.53) | copy-start | bytes 2359300
  174.5 4.8 copy-start.25
  174.8 16.1 %all-to-all-start.3 = ((bf16[1,256,1,12,64]{1,4,2,0,3:T(8,128)(2,1)}), bf16[1,256,1,12,64]{1,4,2,0,3:T(8,128)(2,1)S(1)}, u32[]{:S(2)}, u32[]{:S(2)}) async-start(bf16[1,256,1,12,64]{1,4,2,0,3:T(8,128)(2,1)} %bitcast.40), calls=%async_computation.4 | async-start | bytes 786432 | tf_op jit(solution)/shard_map/all_to_all | solution.py:225
  190.9 31.6 %all-to-all-start = ((bf16[1,256,3,12,64]{1,4,2,0,3:T(8,128)(2,1)}), bf16[1,256,3,12,64]{1,4,2,0,3:T(8,128)(2,1)S(1)}, u32[]{:S(2)}, u32[]{:S(2)}) async-start(bf16[1,256,3,12,64]{1,4,2,0,3:T(8,128)(2,1)} %copy.53), calls=%async_computation | async-start | bytes 2359296 | tf_op jit(solution)/shard_map/all_to_all | solution.py:148
  194.4 82.0 %reduce-scatter.9.cloned.1.call-start = ((), (), s32[]{:S(2)}) async-start(), calls=%async_computation.14 | async-start | bytes 1179648 | tf_op jit(solution)/shard_map/reduce_scatter | solution.py:74
  199.3 135.5 %all-reduce.15.cloned.1.call-start = ((), (), s32[]{:S(2)}) async-start(), calls=%async_computation.19 | async-start | bytes 9437184
  200.8 51.9 %copy-start.9 = (pred[512,1024]{1,0:T(8,128)(4,1)}, pred[512,1024]{1,0:T(8,128)(4,1)S(1)}, u32[]{:S(2)}) copy-start(pred[512,1024]{1,0:T(8,128)(4,1)S(1)} %get-tuple-element.86) | copy-start | bytes 1572868
  200.9 53.9 %copy-start.7 = (pred[512,1024]{1,0:T(8,128)(4,1)}, pred[512,1024]{1,0:T(8,128)(4,1)S(1)}, u32[]{:S(2)}) copy-start(pred[512,1024]{1,0:T(8,128)(4,1)S(1)} %get-tuple-element.85) | copy-start | bytes 1572868
  202.2 3.2 copy-start.21
  202.2 3.2 copy-start.46
  224.3 26.0 %copy-start.11 = (bf16[1,1024,3,3,64]{1,4,3,2,0:T(8,128)(2,1)}, bf16[1,1024,3,3,64]{1,4,3,2,0:T(8,128)(2,1)S(1)}, u32[]{:S(2)}) copy-start(bf16[1,1024,3,3,64]{1,4,3,2,0:T(8,128)(2,1)S(1)} %all_to_all.56) | copy-start | bytes 3538948
  225.7 27.0 %copy-start = (f32[3,512,1024]{2,1,0:T(8,128)}, f32[3,512,1024]{2,1,0:T(8,128)S(1)}, u32[]{:S(2)}) copy-start(f32[3,512,1024]{2,1,0:T(8,128)S(1)} %get-tuple-element.93) | copy-start | bytes 18874372
  229.0 6.4 %copy-start.1 = (f32[3,512,1024]{2,1,0:T(8,128)}, f32[3,512,1024]{2,1,0:T(8,128)S(1)}, u32[]{:S(2)}) copy-start(f32[3,512,1024]{2,1,0:T(8,128)S(1)} %get-tuple-element.95) | copy-start | bytes 18874372
  230.8 4.6 copy-start.42
  266.1 32.4 %all-to-all-start.4 = ((bf16[4,2,73728]{2,1,0:T(2,128)(2,1)}), bf16[4,2,73728]{2,1,0:T(2,128)(2,1)}, u32[]{:S(2)}, u32[]{:S(2)}) async-start(bf16[4,2,73728]{2,1,0:T(2,128)(2,1)} %reshape.772), calls=%async_computation.5 | async-start | bytes 2359296 | tf_op jit(solution)/shard_map/all_to_all | solution.py:70
  270.5 4.6 copy-start.5
  270.5 108.8 %reduce-scatter.7.cloned.1.call-start = ((), (), s32[]{:S(2)}) async-start(), calls=%async_computation.13 | async-start | bytes 1179648 | tf_op jit(solution)/shard_map/reduce_scatter | solution.py:74
  275.1 110.6 %reduce-scatter.13.cloned.1.call-start = ((), (), s32[]{:S(2)}) async-start(), calls=%async_computation.18 | async-start | bytes 245760
  305.7 3.1 copy-start.26
  311.4 3.0 copy-start.45
  314.4 23.7 %copy-start.10 = (pred[512,1024]{1,0:T(8,128)(4,1)S(1)}, pred[512,1024]{1,0:T(8,128)(4,1)}, u32[]{:S(2)}) copy-start(pred[512,1024]{1,0:T(8,128)(4,1)} %copy-done.9) | copy-start | bytes 1572868
  314.4 23.7 %copy-start.12 = (bf16[1,1024,3,3,64]{1,4,3,2,0:T(8,128)(2,1)S(1)}, bf16[1,1024,3,3,64]{1,4,3,2,0:T(8,128)(2,1)}, u32[]{:S(2)}) copy-start(bf16[1,1024,3,3,64]{1,4,3,2,0:T(8,128)(2,1)} %copy-done.11) | copy-start | bytes 3538948
  314.4 23.7 %copy-start.37 = (f32[3,512]{1,0:T(4,128)S(1)}, f32[3,512]{1,0:T(4,128)}, u32[]{:S(2)}) copy-start(f32[3,512]{1,0:T(4,128)} %copy-done.36) | copy-start | bytes 18436
  314.4 23.7 %copy-start.39 = (f32[3,512]{1,0:T(4,128)S(1)}, f32[3,512]{1,0:T(4,128)}, u32[]{:S(2)}) copy-start(f32[3,512]{1,0:T(4,128)} %copy-done.38) | copy-start | bytes 18436
  315.3 150.9 %all-gather.16.cloned.1.call-start = ((), (), s32[]{:S(2)}) async-start(), calls=%async_computation.17 | async-start | bytes 5898240 | tf_op jit(solution)/shard_map/all_gather | solution.py:315
  337.9 5.0 copy-start.8
  338.0 5.0 copy-start.41
  338.0 5.0 copy-start.43
  338.0 186.5 %reduce-scatter.11.cloned.1.call-start = ((), (), s32[]{:S(2)}) async-start(), calls=%async_computation.15 | async-start | bytes 5898240 | tf_op jit(solution)/shard_map/reduce_scatter | solution.py:282
  350.1 21.6 %copy-start.14 = (bf16[256,3,12,64]{0,3,2,1:T(8,128)(2,1)S(1)}, bf16[256,3,12,64]{0,3,2,1:T(8,128)(2,1)}, u32[]{:S(2)}) copy-start(bf16[256,3,12,64]{0,3,2,1:T(8,128)(2,1)} %copy-done.13) | copy-start | bytes 3538948
  350.1 21.7 %copy-start.29 = (f32[256]{0:T(256)S(1)}, f32[256]{0:T(256)}, u32[]{:S(2)}) copy-start(f32[256]{0:T(256)} %copy-done.27) | copy-start | bytes 3076
  350.1 21.7 %copy-start.35 = (f32[256]{0:T(256)S(1)}, f32[256]{0:T(256)}, u32[]{:S(2)}) copy-start(f32[256]{0:T(256)} %copy-done.33) | copy-start | bytes 3076
  375.9 3.4 copy-start.18
  375.9 3.4 copy-start.19
  375.9 8.4 %copy-start.23 = (f32[256,768]{1,0:T(8,128)S(1)}, f32[256,768]{1,0:T(8,128)}, u32[]{:S(2)}) copy-start(f32[256,768]{1,0:T(8,128)} %get-tuple-element.100) | copy-start | bytes 2359300
  375.9 8.4 %copy-start.32 = (f32[768]{0:T(1024)S(1)}, f32[768]{0:T(1024)}, u32[]{:S(2)}) copy-start(f32[768]{0:T(1024)} %copy-done.30) | copy-start | bytes 9220
  376.0 210.8 %all-reduce.13.cloned.1.call-start = ((), (), s32[]{:S(2)}) async-start(), calls=%async_computation.16 | async-start | bytes 2359296 | tf_op jit(solution)/shard_map/psum | solution.py:309
  (16 other events, 34.7 us)
Sparse Core Ops, SparseCore 0:
  9.8 30.3 all-gather.9
  42.1 37.3 all-gather.11
  81.3 37.3 all-gather.13
  120.4 47.2 all-gather.7
  199.4 8.5 reduce-scatter.8
  222.1 112.6 all-reduce.14
  337.6 8.1 reduce-scatter.6
  348.6 25.4 reduce-scatter.12
  376.2 89.9 all-gather.15
  469.0 55.3 reduce-scatter.10
  526.8 59.8 all-reduce.12
